TPU v7x, 32 devices: a whole 2x2x4 slice. The times are simulated.
32 devices in a mesh: pb: 8 (over z, y), ka: 2 (over x), ha: 2 (over core).
Axes of the slice: x: 2, y: 2, z: 4, core: 2. Of those that a mesh axis runs over, the one named last changes fastest.
Arguments:
- queries: bfloat16 [8192, 256], P(('pb', 'ka'), 'ha'), may hold values from -130 to 130
- key_codes: int32 [8192, 256], P(('ka', 'pb'), 'ha'), may hold values from -127 to 127
- value_codes: int32 [8192, 256], P(('ka', 'pb'), 'ha'), may hold values from -127 to 127
- key_scale: float32 [], replicated, may hold values from 0.015 to 0.02
- value_scale: float32 [], replicated, may hold values from 0.01 to 0.02
- out_grad: bfloat16 [8192, 256], P(('pb', 'ka'), 'ha'), may hold values from -256 to 256
Outputs:
- query_grad: float32 [8192, 256], P(('pb', 'ka'), 'ha')
- key_grad: float32 [8192, 256], P(('ka', 'pb'), 'ha')
- value_grad: float32 [8192, 256], P(('ka', 'pb'), 'ha')
All inputs are finite; a program needn't handle non-finite values.
Results may differ from a plain program's by a relative error of at most 0.017.
Values may be sent and summed in bfloat16 or wider, within the bound.
A program may use at most 128 MiB of HBM per device.

v0:
```python
import math

import jax
import jax.numpy as jnp
from jax import lax
from jax.sharding import PartitionSpec as P


def merged(part, axis, combine):
    gathered = jax.tree.map(lambda a: lax.all_gather(a, axis), part)

    def take(source):
        return jax.tree.map(lambda a: lax.dynamic_index_in_dim(a, source, 0, False), gathered)

    return lax.fori_loop(
        1, lax.axis_size(axis), lambda source, state: combine(state, take(source)), take(0)
    )


def dequantize(table, factor):
    return (table.astype(jnp.float32) * factor).astype(jnp.bfloat16)


def contract_last(left, right):
    return lax.dot_general(
        left, right, (((1,), (1,)), ((), ())), preferred_element_type=jnp.float32
    )


def contract_first(left, right):
    return lax.dot_general(
        left, right, (((0,), (0,)), ((), ())), preferred_element_type=jnp.float32
    )


def merge_two(first, second):
    max_a, sum_a = first
    max_b, sum_b = second
    top = jnp.maximum(max_a, max_b)
    return (top, sum_a * jnp.exp(max_a - top) + sum_b * jnp.exp(max_b - top))


def shards(queries, key_codes, value_codes, key_scale, value_scale, out_grad):
    width = queries.shape[1]
    factor = 1.0 / math.sqrt(width)
    q_full, d_full = (
        lax.all_gather(queries, "ka", axis=0, tiled=True),
        lax.all_gather(out_grad, "ka", axis=0, tiled=True),
    )
    key_rows, value_rows = (
        lax.all_gather(key_codes.astype(jnp.bfloat16), "pb", axis=0, tiled=True),
        lax.all_gather(value_codes.astype(jnp.bfloat16), "pb", axis=0, tiled=True),
    )
    keys = dequantize(key_rows, key_scale)
    values = dequantize(value_rows, value_scale)
    rows = q_full.shape[0]
    block_rows = 512
    block_count = rows // block_rows
    q_blocks = q_full.reshape(block_count, block_rows, width)
    d_blocks = d_full.reshape(block_count, block_rows, width)

    def first_pass(totals, inputs):
        q_block, d_block = inputs
        scores = contract_last(q_block, keys) * factor
        row_max = jnp.max(scores, axis=1)
        shifted = jnp.exp(scores - row_max[:, None])
        d_probs = contract_last(d_block, values)
        return (
            totals,
            (
                row_max,
                jnp.sum(shifted, axis=1),
                jnp.sum(shifted * d_probs, axis=1),
                scores,
                d_probs,
            ),
        )

    _, (row_max, row_sum, row_dot, score_tiles, dprob_tiles) = lax.scan(
        first_pass, jnp.float32(0.0), (q_blocks, d_blocks)
    )
    row_max = row_max.reshape(rows)
    row_sum = row_sum.reshape(rows)
    row_dot = row_dot.reshape(rows)
    full_max, full_sum = merged((row_max, row_sum), "ka", merge_two)
    log_total = full_max + jnp.log(full_sum)
    delta_rows = lax.psum(row_dot * jnp.exp(row_max - log_total), "ka")
    lse_blocks = log_total.reshape(block_count, block_rows)
    delta_blocks = delta_rows.reshape(block_count, block_rows)

    def tile_terms(scores, d_probs, lse_block, delta_block):
        probs = jnp.exp(scores - lse_block[:, None])
        d_scores = probs * (d_probs - delta_block[:, None])
        return (probs.astype(jnp.bfloat16), d_scores.astype(jnp.bfloat16))

    def second_full(totals, inputs):
        k_grad, v_grad = totals
        q_block, d_block, scores, d_probs, lse_block, delta_block = inputs
        probs_low, d_scores_low = tile_terms(scores, d_probs, lse_block, delta_block)
        q_grad = jnp.dot(d_scores_low, keys, preferred_element_type=jnp.float32) * factor
        k_grad = k_grad + contract_first(d_scores_low, q_block) * factor
        v_grad = v_grad + contract_first(probs_low, d_block)
        return ((k_grad, v_grad), q_grad)

    inputs = (q_blocks, d_blocks, score_tiles, dprob_tiles, lse_blocks, delta_blocks)
    zeros = jnp.zeros((keys.shape[0], width), jnp.float32)
    (k_grad, v_grad), q_grad = lax.scan(second_full, (zeros, zeros), inputs)
    stacked = jnp.concatenate([k_grad, v_grad], axis=1)
    summed = lax.psum_scatter(
        stacked.astype(jnp.bfloat16), "pb", scatter_dimension=0, tiled=True
    ).astype(jnp.float32)
    key_grad = summed[:, :width]
    value_grad = summed[:, width:]
    query_grad = lax.psum_scatter(
        q_grad.reshape(rows, width).astype(jnp.bfloat16), "ka", scatter_dimension=0, tiled=True
    ).astype(jnp.float32)
    return (query_grad, key_grad, value_grad)


def solution(mesh):
    in_specs = (
        P(("pb", "ka"), "ha"),
        P(("ka", "pb"), "ha"),
        P(("ka", "pb"), "ha"),
        P(),
        P(),
        P(("pb", "ka"), "ha"),
    )
    out_specs = (P(("pb", "ka"), "ha"), P(("ka", "pb"), "ha"), P(("ka", "pb"), "ha"))
    return jax.shard_map(shards, mesh=mesh, in_specs=in_specs, out_specs=out_specs, check_vma=False)
```

profile of v0, /device:TPU:0, one launch (start us, length us, event | category | flops | bytes accessed | tf_op | source)
XLA Modules:
  0.0 266.3 jit_solution(2322853706921836254)
XLA Ops:
  7.2 0.0 all-gather.5.cloned.1.call-start
  7.2 1.6 convert_element_type.45
  8.8 0.0 all-gather.5.cloned.1.call-update
  8.9 0.0 all-gather.7.cloned.1.call-start
  8.9 1.6 convert_element_type.48
  10.5 0.0 all-gather.7.cloned.1.call-update
  10.6 0.0 reduce-scatter.3.cloned.1.call-start
  12.0 7.4 %all_gather.18 = bf16[1024,128]{1,0:T(8,128)(2,1)S(1)} all-gather(bf16[512,128]{1,0:T(8,128)(2,1)} %param.10), channel_id=1, replica_groups=mesh['pb'=8,'ka'=2,'ha'=2] {'ka'}, dimensions={0}, use_global_device_ids=true | all-gather | bytes 393216 | tf_op jit(solution)/shard_map/all_gather | solution.py:47
  19.3 7.2 %all_gather.20 = bf16[1024,128]{1,0:T(8,128)(2,1)} all-gather(bf16[512,128]{1,0:T(8,128)(2,1)} %param.15), channel_id=1, replica_groups=mesh['pb'=8,'ka'=2,'ha'=2] {'ka'}, dimensions={0}, use_global_device_ids=true | all-gather | bytes 393216 | tf_op jit(solution)/shard_map/all_gather | solution.py:48
  26.5 27.2 %all-gather.5.cloned.1.call-done = bf16[4096,128]{1,0:T(8,128)(2,1)} async-done(((bf16[512,128]{1,0:T(8,128)(2,1)}), bf16[4096,128]{1,0:T(8,128)(2,1)}) %all-gather.5.cloned.1.call-update) | async-done | bytes 1048592 | tf_op jit(solution)/shard_map/all_gather | solution.py:51
  53.6 1.4 multiply_convert_fusion.2
  55.1 40.2 %all-gather.7.cloned.1.call-done = bf16[4096,128]{1,0:T(8,128)(2,1)} async-done(((bf16[512,128]{1,0:T(8,128)(2,1)}), bf16[4096,128]{1,0:T(8,128)(2,1)}) %all-gather.7.cloned.1.call-update) | async-done | bytes 1048592 | tf_op jit(solution)/shard_map/all_gather | solution.py:52
  95.3 2.4 multiply_convert_fusion.1
  97.7 21.8 %while.13 = (s32[]{:T(128)}, f32[2,512]{1,0:T(2,128)S(1)}, f32[2,512]{1,0:T(2,128)S(1)}, f32[2,512]{1,0:T(2,128)S(1)}, f32[2,512,4096]{2,1,0:T(8,128)}, /*index=...) while((s32[]{:T(128)}, f32[2,512]{1,0:T(2,128)S(1)}, ...), condition=%wide.region_4.5_spmd, body=%wide.region_0.4_spmd.sunk | while | flops 1090517504 | bytes 66343616 | solution.py:79
  97.7 0.0 copy-start.1
  97.7 0.0 copy-start.2
  97.7 1.3 multiply_reduce_fusion.4
  99.0 0.0 copy-done.1
  99.0 0.0 copy-done.2
  99.0 3.0 %multiply_reduce_fusion.5 = (f32[512]{0:T(512)S(1)}, f32[512]{0:T(512)S(1)}, f32[512,4096]{1,0:T(8,128)S(1)}) fusion(f32[512,4096]{1,0:T(8,128)S(1)} %get-tuple-element.372, f32[512]{0:T(512)S(1)} %get-tuple-element.371, bf16[4096,128]{1,0:T(8,128)(2,1)S(1)} %copy-done.1, bf16[2,512,128]{2,1,0:T(8,128)(2,1)S(1)} %copy-done.2, s32[]{:T(128)} %get-tuple-element.403), kind=kOutput, calls=%fused_computation.2.clone.1 | convolution fusion | flops 547355648 | bytes 17963012 | tf_op jit(solution)/shard_map/while/body/eval_jaxpr/dot_general | solution.py:25
  102.0 6.4 %bitcast_dynamic-update-slice_fusion.3 = (f32[2,512,4096]{2,1,0:T(8,128)}, f32[2,512,4096]{2,1,0:T(8,128)}) fusion(f32[2,512,4096]{2,1,0:T(8,128)} %get-tuple-element.408, s32[]{:T(128)} %get-tuple-element.403, f32[512,4096]{1,0:T(8,128)S(1)} %get-tuple-element.375, f32[2,512,4096]{2,1,0:T(8,128)} %get-tuple-element.407, ...), kind=kLoop, calls=%fused_computation.clone.1 | loop fusion | flops 2097152 | bytes 33554944 | tf_op jit(solution)/shard_map/while/body/jit(dynamic_update_index_in_dim)/dynamic_update_slice | solution.py:79
  108.6 0.0 copy-start.1
  108.6 0.0 copy-start.2
  108.6 1.3 multiply_reduce_fusion.4
  109.9 0.0 copy-done.1
  109.9 0.0 copy-done.2
  109.9 3.0 %multiply_reduce_fusion.5 = (f32[512]{0:T(512)S(1)}, f32[512]{0:T(512)S(1)}, f32[512,4096]{1,0:T(8,128)S(1)}) fusion(f32[512,4096]{1,0:T(8,128)S(1)} %get-tuple-element.372, f32[512]{0:T(512)S(1)} %get-tuple-element.371, bf16[4096,128]{1,0:T(8,128)(2,1)S(1)} %copy-done.1, bf16[2,512,128]{2,1,0:T(8,128)(2,1)S(1)} %copy-done.2, s32[]{:T(128)} %get-tuple-element.403), kind=kOutput, calls=%fused_computation.2.clone.1 | convolution fusion | flops 547355648 | bytes 17963012 | tf_op jit(solution)/shard_map/while/body/eval_jaxpr/dot_general | solution.py:25
  112.9 6.4 %bitcast_dynamic-update-slice_fusion.3 = (f32[2,512,4096]{2,1,0:T(8,128)}, f32[2,512,4096]{2,1,0:T(8,128)}) fusion(f32[2,512,4096]{2,1,0:T(8,128)} %get-tuple-element.408, s32[]{:T(128)} %get-tuple-element.403, f32[512,4096]{1,0:T(8,128)S(1)} %get-tuple-element.375, f32[2,512,4096]{2,1,0:T(8,128)} %get-tuple-element.407, ...), kind=kLoop, calls=%fused_computation.clone.1 | loop fusion | flops 2097152 | bytes 33554944 | tf_op jit(solution)/shard_map/while/body/jit(dynamic_update_index_in_dim)/dynamic_update_slice | solution.py:79
  119.5 4.3 %all-gather = f32[2,1,1024]{2,1,0:T(1,128)S(1)} all-gather(f32[1,1,1024]{2,1,0:T(1,128)S(1)} %reshape.58), channel_id=1, replica_groups=mesh['pb'=8,'ka'=2,'ha'=2] {'ka'}, dimensions={0}, use_global_device_ids=true | all-gather | bytes 12288 | tf_op jit(solution)/shard_map/all_gather | solution.py:10
  123.8 4.3 %all-gather.1 = f32[2,1,1024]{2,1,0:T(1,128)S(1)} all-gather(f32[1,1,1024]{2,1,0:T(1,128)S(1)} %reshape.60), channel_id=1, replica_groups=mesh['pb'=8,'ka'=2,'ha'=2] {'ka'}, dimensions={0}, use_global_device_ids=true | all-gather | bytes 12288 | tf_op jit(solution)/shard_map/all_gather | solution.py:10
  128.2 4.9 %psum.7 = f32[2,512]{1,0:T(2,128)S(1)} all-reduce(f32[2,512]{1,0:T(2,128)S(1)} %reshape.57), channel_id=1, replica_groups=mesh['pb'=8,'ka'=2,'ha'=2] {'ka'}, use_global_device_ids=true, to_apply=%region_5.6 | all-reduce | flops 1024 | bytes 8192 | tf_op jit(solution)/shard_map/psum | solution.py:87
  133.3 42.3 %while.40 = (s32[]{:T(128)}, f32[4096,128]{1,0:T(8,128)S(1)}, f32[4096,128]{1,0:T(8,128)}, bf16[2,512,128]{2,1,0:T(8,128)(2,1)}, f32[2,512,4096]{2,1,0:T(8,128)}...) while((s32[]{:T(128)}, f32[4096,128]{1,0:T(8,128)S(1)}, ...), condition=%wide.region_7.8_spmd.clone, body=%wide.region_6.7_spmd.clone.sunk | while | flops 1634271232 | bytes 122180872 | solution.py:107
  133.3 0.0 copy-start
  133.3 0.0 copy-start.4
  133.3 9.4 %fusion.65 = f32[4096,128]{1,0:T(8,128)S(1)} fusion(f32[2,512,4096]{2,1,0:T(8,128)} %get-tuple-element.459, s32[]{:T(128)} %get-tuple-element.440, f32[2,512,4096]{2,1,0:T(8,128)} %get-tuple-element.457, f32[512]{0:T(512)S(1)} %bitcast.117, f32[512]{0:T(512)S(1)} %bitcast.114, f32[4096,128]{1,0:T(8,128)S(1)} %get-tuple-element.441, ...), kind=kOutput, calls=%fused_computation.24.clone.1 | convolution fusion | flops 546832384 | bytes 21107712 | tf_op jit(solution)/shard_map/while/body/eval_jaxpr/dot_general | solution.py:31
  142.7 1.2 copy-done
  143.8 0.0 copy-done.4
  143.8 0.0 copy-start.3
  143.8 5.5 %fusion.66 = bf16[2,512,128]{2,1,0:T(8,128)(2,1)S(1)} fusion(bf16[2,512,128]{2,1,0:T(8,128)(2,1)S(1)} %copy-done.4, s32[]{:T(128)} %get-tuple-element.440, bf16[4096,128]{1,0:T(8,128)(2,1)S(1)} %get-tuple-element.463, f32[2,512,4096]{2,1,0:T(8,128)} %get-tuple-element.459, f32[2,512,4096]{2,1,0:T(8,128)S(1)} %copy-done, f32[512]{0:T(512)S(1)} %bitcast.118, ...), kind=kOutput, calls=%fused_computation.33.clone.1 | convolution fusion | flops 545325056 | bytes 18093056 | tf_op jit(solution)/shard_map/while/body/eval_jaxpr/dot_general | solution.py:100
  149.3 0.0 copy-start.5
  149.3 0.7 copy-done.5
  150.0 0.0 copy-done.3
  150.0 3.6 %convolution_add_fusion.2 = f32[4096,128]{1,0:T(8,128)} fusion(f32[2,512,4096]{2,1,0:T(8,128)S(1)} %copy-done, s32[]{:T(128)} %get-tuple-element.440, f32[512]{0:T(512)S(1)} %bitcast.116, f32[4096,128]{1,0:T(8,128)} %get-tuple-element.442, pred[]{:T(512)S(6)} %compare.3, bf16[2,512,128]{2,1,0:T(8,128)(2,1)S(1)} %copy-done.3), kind=kOutput, calls=%fused_computation.22.clone.1 | convolution fusion | flops 542113792 | bytes 12717057 | tf_op jit(solution)/shard_map/while/body/eval_jaxpr/dot_general | solution.py:31
  153.6 0.0 copy-start
  153.7 0.0 copy-start.4
  153.7 9.4 %fusion.65 = f32[4096,128]{1,0:T(8,128)S(1)} fusion(f32[2,512,4096]{2,1,0:T(8,128)} %get-tuple-element.459, s32[]{:T(128)} %get-tuple-element.440, f32[2,512,4096]{2,1,0:T(8,128)} %get-tuple-element.457, f32[512]{0:T(512)S(1)} %bitcast.117, f32[512]{0:T(512)S(1)} %bitcast.114, f32[4096,128]{1,0:T(8,128)S(1)} %get-tuple-element.441, ...), kind=kOutput, calls=%fused_computation.24.clone.1 | convolution fusion | flops 546832384 | bytes 21107712 | tf_op jit(solution)/shard_map/while/body/eval_jaxpr/dot_general | solution.py:31
  163.0 1.2 copy-done
  164.2 0.0 copy-done.4
  164.2 0.0 copy-start.3
  164.2 5.5 %fusion.66 = bf16[2,512,128]{2,1,0:T(8,128)(2,1)S(1)} fusion(bf16[2,512,128]{2,1,0:T(8,128)(2,1)S(1)} %copy-done.4, s32[]{:T(128)} %get-tuple-element.440, bf16[4096,128]{1,0:T(8,128)(2,1)S(1)} %get-tuple-element.463, f32[2,512,4096]{2,1,0:T(8,128)} %get-tuple-element.459, f32[2,512,4096]{2,1,0:T(8,128)S(1)} %copy-done, f32[512]{0:T(512)S(1)} %bitcast.118, ...), kind=kOutput, calls=%fused_computation.33.clone.1 | convolution fusion | flops 545325056 | bytes 18093056 | tf_op jit(solution)/shard_map/while/body/eval_jaxpr/dot_general | solution.py:100
  169.7 0.0 copy-start.5
  169.7 0.7 copy-done.5
  170.4 0.0 copy-done.3
  170.4 5.2 %convolution_add_fusion.2 = f32[4096,128]{1,0:T(8,128)} fusion(f32[2,512,4096]{2,1,0:T(8,128)S(1)} %copy-done, s32[]{:T(128)} %get-tuple-element.440, f32[512]{0:T(512)S(1)} %bitcast.116, f32[4096,128]{1,0:T(8,128)} %get-tuple-element.442, pred[]{:T(512)S(6)} %compare.3, bf16[2,512,128]{2,1,0:T(8,128)(2,1)S(1)} %copy-done.3), kind=kOutput, calls=%fused_computation.22.clone.1 | convolution fusion | flops 542113792 | bytes 12717057 | tf_op jit(solution)/shard_map/while/body/eval_jaxpr/dot_general | solution.py:31
  175.6 0.0 reduce-scatter.3.cloned.1.call-update
  175.6 0.0 reduce-scatter.5.cloned.1.call-start
  175.6 0.1 convert.6
  175.8 1.7 convert.7
  177.5 1.6 pad_maximum_fusion
  179.0 0.0 reduce-scatter.5.cloned.1.call-update
  179.1 7.1 %reduce-scatter.3.cloned.1.call-done = bf16[512,128]{1,0:T(8,128)(2,1)} async-done(((bf16[1024,128]{1,0:T(8,128)(2,1)}), bf16[512,128]{1,0:T(8,128)(2,1)}) %reduce-scatter.3.cloned.1.call-update) | async-done | bytes 131088 | tf_op jit(solution)/shard_map/reduce_scatter | solution.py:114
  186.2 1.6 convert_element_type.53
  187.8 70.2 %reduce-scatter.5.cloned.1.call-done = bf16[512,256]{1,0:T(8,128)(2,1)} async-done(((bf16[4096,256]{1,0:T(8,128)(2,1)}), bf16[512,256]{1,0:T(8,128)(2,1)}) %reduce-scatter.5.cloned.1.call-update) | async-done | bytes 262160 | tf_op jit(solution)/shard_map/reduce_scatter | solution.py:109
  258.0 1.8 fusion.43
  (28 shorter events, 0.4 us)
Async XLA Ops:
  7.2 46.5 %all-gather.5.cloned.1.call-start = ((), (), s32[]{:S(2)}) async-start(), calls=%async_computation.2 | async-start | bytes 1179648 | tf_op jit(solution)/shard_map/all_gather | solution.py:51
  8.9 86.4 %all-gather.7.cloned.1.call-start = ((), (), s32[]{:S(2)}) async-start(), calls=%async_computation.3 | async-start | bytes 1179648 | tf_op jit(solution)/shard_map/all_gather | solution.py:52
  10.6 175.6 %reduce-scatter.3.cloned.1.call-start = ((), (), s32[]{:S(2)}) async-start(), calls=%async_computation.4 | async-start | bytes 393216 | tf_op jit(solution)/shard_map/reduce_scatter | solution.py:114
  97.7 1.3 copy-start.1
  97.7 1.3 copy-start.2
  108.6 1.4 copy-start.1
  108.6 1.4 copy-start.2
  133.3 10.5 %copy-start = (f32[2,512,4096]{2,1,0:T(8,128)S(1)}, f32[2,512,4096]{2,1,0:T(8,128)}, u32[]{:S(2)}) copy-start(f32[2,512,4096]{2,1,0:T(8,128)} %get-tuple-element.457) | copy-start | bytes 50331652 | tf_op jit(solution)/shard_map/while
  133.3 10.5 %copy-start.4 = (bf16[2,512,128]{2,1,0:T(8,128)(2,1)S(1)}, bf16[2,512,128]{2,1,0:T(8,128)(2,1)}, u32[]{:S(2)}) copy-start(bf16[2,512,128]{2,1,0:T(8,128)(2,1)} %get-tuple-element.443) | copy-start | bytes 786436 | tf_op jit(solution)/shard_map/while
  143.8 6.2 %copy-start.3 = (bf16[2,512,128]{2,1,0:T(8,128)(2,1)S(1)}, bf16[2,512,128]{2,1,0:T(8,128)(2,1)}, u32[]{:S(2)}) copy-start(bf16[2,512,128]{2,1,0:T(8,128)(2,1)} %get-tuple-element.462) | copy-start | bytes 786436 | tf_op jit(solution)/shard_map/while
  149.3 0.7 copy-start.5
  153.6 10.5 %copy-start = (f32[2,512,4096]{2,1,0:T(8,128)S(1)}, f32[2,512,4096]{2,1,0:T(8,128)}, u32[]{:S(2)}) copy-start(f32[2,512,4096]{2,1,0:T(8,128)} %get-tuple-element.457) | copy-start | bytes 50331652 | tf_op jit(solution)/shard_map/while
  153.7 10.5 %copy-start.4 = (bf16[2,512,128]{2,1,0:T(8,128)(2,1)S(1)}, bf16[2,512,128]{2,1,0:T(8,128)(2,1)}, u32[]{:S(2)}) copy-start(bf16[2,512,128]{2,1,0:T(8,128)(2,1)} %get-tuple-element.443) | copy-start | bytes 786436 | tf_op jit(solution)/shard_map/while
  164.2 6.2 %copy-start.3 = (bf16[2,512,128]{2,1,0:T(8,128)(2,1)S(1)}, bf16[2,512,128]{2,1,0:T(8,128)(2,1)}, u32[]{:S(2)}) copy-start(bf16[2,512,128]{2,1,0:T(8,128)(2,1)} %get-tuple-element.462) | copy-start | bytes 786436 | tf_op jit(solution)/shard_map/while
  169.7 0.7 copy-start.5
  175.6 82.4 %reduce-scatter.5.cloned.1.call-start = ((), (), s32[]{:S(2)}) async-start(), calls=%async_computation.5 | async-start | bytes 2359296 | tf_op jit(solution)/shard_map/reduce_scatter | solution.py:109
Sparse Core Ops, SparseCore 0:
  10.7 42.9 all-gather.4
  56.3 38.8 all-gather.6
  175.7 10.4 reduce-scatter.2
  190.0 67.9 reduce-scatter.4
where the time goes:
time: 267 us; the launch traced here: 266 us
  waiting for transfers between devices  145 us (54%)
  matrix products  47.1 us (18%)
  blocking collectives  28.1 us (11%)
  other arithmetic  24.9 us (9%)
  between operations  15.2 us (6%)
  local copies, waits for them, and re-layouts  5.91 us (2%)
    reduce_scatter x1, waiting for transfers between devices, shards(): lax.psum_scatter(stacked.astype(jnp.bfloat16), 'pb', scatter_dimension=0,...  70.2 us
    all_gather x1, waiting for transfers between devices, shards(): lax.all_gather(value_codes.astype(jnp.bfloat16), 'pb', axis=0, tiled=True)  40.2 us
    dot_general x4, matrix products, contract_first(): lax.dot_general(left, right, (((0,), (0,)), ((), ())), preferred_element_...  27.5 us
    all_gather x1, waiting for transfers between devices, shards(): lax.all_gather(key_codes.astype(jnp.bfloat16), 'pb', axis=0, tiled=True)  27.2 us
    dynamic_update_slice x2, other arithmetic, shards(): lax.scan(first_pass, jnp.float32(0.0), (q_blocks, d_blocks))  12.8 us
    dot_general x2, matrix products, second_full(): jnp.dot(d_scores_low, keys, preferred_element_type=jnp.float32) * factor  11 us
    all_gather x2, blocking collectives, merged(): gathered = jax.tree.map(lambda a: lax.all_gather(a, axis), part)  8.68 us
    dot_general x4, matrix products, contract_last(): lax.dot_general(left, right, (((1,), (1,)), ((), ())), preferred_element_...  8.63 us
  transfers between devices with their start and end apart: 4, of which 4 were waited for; matrix products, arithmetic and copies ran while one was open for 3% of the time, Pallas kernels for 0%

commit v1 on v0

v1 whole, which is shorter than its diff:
```python
import functools
import math

import jax
import jax.numpy as jnp
from jax import lax
from jax.experimental import pallas as pl
from jax.experimental.pallas import tpu as pltpu
from jax.sharding import PartitionSpec as P

MESH = pl.DeviceIdType.MESH
LOW = jnp.bfloat16
WIDE = jnp.float32


def flipped(rank, step, count):
    total = 0
    bit = 1
    while bit < count:
        one = (rank // bit) % 2
        two = (step // bit) % 2
        total = total + bit * (one + two - 2 * one * two)
        bit *= 2
    return total


def contract(left, right, dims):
    return lax.dot_general(left, right, ((dims[:1], dims[1:]), ((), ())), preferred_element_type=WIDE)


def kernel(
    nq, nk, nka, fold,
    key_scale, value_scale, q_ref, g_ref, kc_ref, vc_ref,
    dq_ref, dk_ref, dv_ref,
    qd, kv, stats, lse, delta, acc_q, acc_k, acc_v,
    gk_out, gk_in, gq_out, gq_in,
    q_send, q_recv, k_send, k_recv, s_send, s_recv, gk_send, gk_recv, gq_send, gq_recv,
):
    rows, width = q_ref.shape
    factor = 1.0 / math.sqrt(width)
    log2e = math.log2(math.e)
    pb, ka = lax.axis_index("pb"), lax.axis_index("ka")
    my_q = pb // fold
    low = pb % fold
    my_k = low * nka + ka

    def q_peer(rank):
        return {"pb": rank * fold + low, "ka": ka}

    def k_peer(rank):
        return {"pb": my_q * fold + rank // nka, "ka": rank % nka}

    def q_copy(rank, slot):
        return pltpu.make_async_remote_copy(
            qd.at[slot], qd.at[slot], q_send.at[rank], q_recv.at[slot],
            device_id=q_peer(rank), device_id_type=MESH)

    def k_copy(rank, slot):
        return pltpu.make_async_remote_copy(
            kv.at[slot], kv.at[slot], k_send.at[rank], k_recv.at[slot],
            device_id=k_peer(rank), device_id_type=MESH)

    def s_copy(rank, slot):
        return pltpu.make_async_remote_copy(
            stats.at[slot], stats.at[slot], s_send.at[rank], s_recv.at[slot],
            device_id=q_peer(rank), device_id_type=MESH)

    def gk_copy(rank, slot):
        return pltpu.make_async_remote_copy(
            gk_out.at[rank], gk_in.at[slot], gk_send.at[rank], gk_recv.at[slot],
            device_id=k_peer(rank), device_id_type=MESH)

    def gq_copy(rank, slot):
        return pltpu.make_async_remote_copy(
            gq_out.at[rank], gq_in.at[slot], gq_send.at[rank], gq_recv.at[slot],
            device_id=q_peer(rank), device_id_type=MESH)

    barrier = pltpu.get_barrier_semaphore()
    for step in range(1, nq):
        pl.semaphore_signal(barrier, inc=1, device_id=q_peer(flipped(my_q, step, nq)), device_id_type=MESH)
    for step in range(1, nk):
        pl.semaphore_signal(barrier, inc=1, device_id=k_peer(flipped(my_k, step, nk)), device_id_type=MESH)
    qd[my_q, 0] = q_ref[...]
    qd[my_q, 1] = g_ref[...]
    kv[my_k, 0] = (kc_ref[...].astype(WIDE) * key_scale[0]).astype(LOW)
    kv[my_k, 1] = (vc_ref[...].astype(WIDE) * value_scale[0]).astype(LOW)
    pl.semaphore_wait(barrier, nq + nk - 2)

    for step in range(1, nq):
        q_copy(flipped(my_q, step, nq), my_q).start()
    for step in range(1, nk):
        k_copy(flipped(my_k, step, nk), my_k).start()

    @pl.loop(0, nq)
    def _(jj):
        j = flipped(my_q, jj, nq)

        @pl.when(jj > 0)
        def _():
            q_copy(j, j).wait_recv()

        def step_keys(ii, state):
            top, total, dot = state
            i = flipped(my_k, ii, nk)

            @pl.when((jj == 0) & (ii > 0))
            def _():
                k_copy(i, i).wait_recv()

            scores = contract(kv[i, 0], qd[j, 0], (1, 1)) * (factor * log2e)
            d_probs = contract(kv[i, 1], qd[j, 1], (1, 1))
            new_top = jnp.maximum(top, jnp.max(scores, axis=0, keepdims=True))
            shifted = jnp.exp2(scores - new_top)
            old = jnp.exp2(top - new_top)
            total = total * old + jnp.sum(shifted, axis=0, keepdims=True)
            dot = dot * old + jnp.sum(shifted * d_probs, axis=0, keepdims=True)
            return new_top, total, dot

        zero = jnp.zeros((1, rows), WIDE)
        top, total, dot = lax.fori_loop(0, nk, step_keys, (zero - 1e30, zero, zero))
        stats[my_q, pl.ds(j, 1), :] = top + jnp.log2(total)
        stats[my_q, pl.ds(nq + j, 1), :] = dot / total

    for step in range(1, nq):
        s_copy(flipped(my_q, step, nq), my_q).start()
    for step in range(1, nq):
        other = flipped(my_q, step, nq)
        s_copy(other, other).wait_recv()
    parts = [stats[r, 0:nq, :] for r in range(nq)]
    best = functools.reduce(jnp.maximum, parts)
    weights = [jnp.exp2(part - best) for part in parts]
    whole = sum(weights)
    lse[...] = best + jnp.log2(whole)
    delta[...] = sum(w * stats[r, nq : 2 * nq, :] for r, w in enumerate(weights)) / whole

    acc_q[...] = jnp.zeros_like(acc_q)

    @pl.loop(1, nk + 1)
    def _(ii):
        i = flipped(my_k, ii % nk, nk)
        acc_k[...] = jnp.zeros_like(acc_k)
        acc_v[...] = jnp.zeros_like(acc_v)

        @pl.loop(1, nq + 1)
        def _(jj):
            j = flipped(my_q, jj % nq, nq)
            keys, queries, grads = kv[i, 0], qd[j, 0], qd[j, 1]
            scores = contract(keys, queries, (1, 1)) * (factor * log2e)
            d_probs = contract(kv[i, 1], grads, (1, 1))
            probs = jnp.exp2(scores - lse[pl.ds(j, 1), :])
            d_scores = (probs * (d_probs - delta[pl.ds(j, 1), :])).astype(LOW)
            acc_v[...] += contract(probs.astype(LOW), grads, (1, 0))
            acc_k[...] += contract(d_scores, queries, (1, 0))
            acc_q[j] += contract(d_scores, keys, (0, 0))

            @pl.when((ii == nk) & (jj < nq))
            def _():
                gq_out[j] = (acc_q[j] * factor).astype(LOW)
                gq_copy(j, my_q).start()

        @pl.when(ii < nk)
        def _():
            gk_out[i, 0] = (acc_k[...] * factor).astype(LOW)
            gk_out[i, 1] = acc_v[...].astype(LOW)
            gk_copy(i, my_k).start()

    key_sum, value_sum = acc_k[...] * factor, acc_v[...]
    for step in range(1, nk):
        other = flipped(my_k, step, nk)
        gk_copy(other, other).wait_recv()
        key_sum = key_sum + gk_in[other, 0].astype(WIDE)
        value_sum = value_sum + gk_in[other, 1].astype(WIDE)
    dk_ref[...] = key_sum
    dv_ref[...] = value_sum
    query_sum = acc_q[my_q] * factor
    for step in range(1, nq):
        other = flipped(my_q, step, nq)
        gq_copy(other, other).wait_recv()
        query_sum = query_sum + gq_in[other].astype(WIDE)
    dq_ref[...] = query_sum
    for step in range(1, nq):
        other = flipped(my_q, step, nq)
        q_copy(other, my_q).wait_send()
        s_copy(other, my_q).wait_send()
        gq_copy(other, my_q).wait_send()
    for step in range(1, nk):
        other = flipped(my_k, step, nk)
        k_copy(other, my_k).wait_send()
        gk_copy(other, my_k).wait_send()


def shards(queries, key_codes, value_codes, key_scale, value_scale, out_grad):
    rows, width = queries.shape
    npb, nka = lax.axis_size("pb"), lax.axis_size("ka")
    fold = 2
    nq, nk = npb // fold, fold * nka
    vmem = pl.BlockSpec(memory_space=pltpu.VMEM)
    smem = pl.BlockSpec(memory_space=pltpu.SMEM)
    out = jax.ShapeDtypeStruct((rows, width), WIDE)
    sems = [pltpu.SemaphoreType.DMA((n,)) for n in (nq, nq, nk, nk, nq, nq, nk, nk, nq, nq)]
    return tuple(
        pl.pallas_call(
            functools.partial(kernel, nq, nk, nka, fold),
            out_shape=(out, out, out),
            in_specs=[smem, smem, vmem, vmem, vmem, vmem],
            out_specs=(vmem, vmem, vmem),
            scratch_shapes=[
                pltpu.VMEM((nq, 2, rows, width), LOW),
                pltpu.VMEM((nk, 2, rows, width), LOW),
                pltpu.VMEM((nq, 2 * nq, rows), WIDE),
                pltpu.VMEM((nq, rows), WIDE),
                pltpu.VMEM((nq, rows), WIDE),
                pltpu.VMEM((nq, rows, width), WIDE),
                pltpu.VMEM((rows, width), WIDE),
                pltpu.VMEM((rows, width), WIDE),
                pltpu.VMEM((nk, 2, rows, width), LOW),
                pltpu.VMEM((nk, 2, rows, width), LOW),
                pltpu.VMEM((nq, rows, width), LOW),
                pltpu.VMEM((nq, rows, width), LOW),
                *sems,
            ],
            compiler_params=pltpu.CompilerParams(
                collective_id=0, has_side_effects=True, vmem_limit_bytes=48 << 20
            ),
        )(key_scale.reshape(1), value_scale.reshape(1), queries, out_grad, key_codes, value_codes)
    )


def solution(mesh):
    in_specs = (
        P(("pb", "ka"), "ha"),
        P(("ka", "pb"), "ha"),
        P(("ka", "pb"), "ha"),
        P(),
        P(),
        P(("pb", "ka"), "ha"),
    )
    out_specs = (P(("pb", "ka"), "ha"), P(("ka", "pb"), "ha"), P(("ka", "pb"), "ha"))
    return jax.shard_map(shards, mesh=mesh, in_specs=in_specs, out_specs=out_specs, check_vma=False)
```

time: 267 us -> 65.4 us (0.24)
  waiting for transfers between devices: 145 us -> 0 us
  Pallas kernels: 0 us -> 57.4 us
  matrix products: 47.1 us -> 0 us
  blocking collectives: 28.1 us -> 0 us
  other arithmetic: 24.9 us -> 0 us
  between operations: 15.2 us -> 1.94 us
    reduce_scatter x2 -> x0, waiting for transfers between devices: 77.3 us -> none  [the longest x1 70.2 us: shards(): lax.psum_scatter(stacked.astype(jnp.bfloat16), 'pb', scatter_dimension=0,...]
    all_gather x2 -> x0, waiting for transfers between devices: 67.4 us -> none  [the longest x1 40.2 us: shards(): lax.all_gather(value_codes.astype(jnp.bfloat16), 'pb', axis=0, tiled=True)]
    pallas_call x0 -> x1, Pallas kernels: none -> 57.4 us  [shards(): pl.pallas_call(functools.partial(kernel, nq, nk, nka, fold), out_shape=(o...]
    dot_general x10 -> x0, matrix products: 47.1 us -> none  [the longest x4 27.5 us: contract_first(): lax.dot_general(left, right, (((0,), (0,)), ((), ())), preferred_element_...]
    all_gather x4 -> x0, blocking collectives: 23.2 us -> none  [the longest x2 8.68 us: merged(): gathered = jax.tree.map(lambda a: lax.all_gather(a, axis), part)]
    dynamic_update_slice x2 -> x0, other arithmetic: 12.8 us -> none  [shards(): lax.scan(first_pass, jnp.float32(0.0), (q_blocks, d_blocks))]
    convert_element_type x5 -> x0, other arithmetic: 8.7 us -> none  [the longest x2 3.84 us: dequantize(): return (table.astype(jnp.float32) * factor).astype(jnp.bfloat16)]
    unnamed x4 -> x11, local copies, waits for them, and re-layouts: 0.04 us -> 5.81 us
  transfers between devices with their start and end apart: 4 -> 0, of which waited for: 4 -> 0; matrix products, arithmetic and copies ran while one was open for 3% -> 0% of each run, Pallas kernels for 0% -> 0%
where the time goes in v1:
time: 65.4 us; the launch traced here: 65.1 us
  Pallas kernels  57.4 us (88%)
  local copies, waits for them, and re-layouts  5.81 us (9%)
  between operations  1.94 us (3%)
    pallas_call x1, Pallas kernels, shards(): pl.pallas_call(functools.partial(kernel, nq, nk, nka, fold), out_shape=(o...  57.4 us
    unnamed x11, local copies, waits for them, and re-layouts  5.81 us

profile of v1, /device:TPU:0, one launch (start us, length us, event | category | flops | bytes accessed | tf_op | source)
XLA Modules:
  0.0 65.1 jit_solution(8957467429372166886)
XLA Ops:
  1.9 0.0 copy-start
  1.9 0.9 %copy-done = s32[512,128]{1,0:T(8,128)S(1)} copy-done((s32[512,128]{1,0:T(8,128)S(1)}, s32[512,128]{1,0:T(8,128)}, u32[]{:S(2)}) %copy-start) | copy-done | bytes 262168
  2.9 0.0 copy-start.1
  2.9 0.9 %copy-done.1 = s32[512,128]{1,0:T(8,128)S(1)} copy-done((s32[512,128]{1,0:T(8,128)S(1)}, s32[512,128]{1,0:T(8,128)}, u32[]{:S(2)}) %copy-start.1) | copy-done | bytes 262168
  3.8 0.0 copy-start.2
  3.8 0.9 %copy-done.2 = bf16[512,128]{1,0:T(8,128)(2,1)S(1)} copy-done((bf16[512,128]{1,0:T(8,128)(2,1)S(1)}, bf16[512,128]{1,0:T(8,128)(2,1)}, u32[]{:S(2)}) %copy-start.2) | copy-done | bytes 131096
  4.7 0.0 copy-start.3
  4.7 0.9 %copy-done.3 = bf16[512,128]{1,0:T(8,128)(2,1)S(1)} copy-done((bf16[512,128]{1,0:T(8,128)(2,1)S(1)}, bf16[512,128]{1,0:T(8,128)(2,1)}, u32[]{:S(2)}) %copy-start.3) | copy-done | bytes 131096
  5.6 57.4 %shard_map.85 = (f32[512,128]{1,0:T(8,128)S(1)}, f32[512,128]{1,0:T(8,128)S(1)}, f32[512,128]{1,0:T(8,128)S(1)}) custom-call(f32[1]{0:T(128)} %bitcast.2.key_scale, f32[1]{0:T(128)} %bitcast.3.value_scale, bf16[512,128]{1,0:T(8,128)(2,1)S(1)} %copy-done.2, bf16[512,128]{1,0:T(8,128)(2,1)S(1)} %copy-done.3, s32[512,128]{1,0:T(8,128)S(1)} %copy-done, ...), custom_call_target="tpu_custom_call" | custom-call | tf_op jit(solution)/shard_map/pallas_call | solution.py:202
  63.0 0.7 %copy.14 = f32[512,128]{1,0:T(8,128)} copy(f32[512,128]{1,0:T(8,128)S(1)} %get-tuple-element.6) | data formatting | bytes 524288
  63.7 0.7 %copy.15 = f32[512,128]{1,0:T(8,128)} copy(f32[512,128]{1,0:T(8,128)S(1)} %get-tuple-element.7) | data formatting | bytes 524288
  64.4 0.7 %copy.16 = f32[512,128]{1,0:T(8,128)} copy(f32[512,128]{1,0:T(8,128)S(1)} %get-tuple-element.8) | data formatting | bytes 524288
Async XLA Ops:
  1.9 1.0 %copy-start = (s32[512,128]{1,0:T(8,128)S(1)}, s32[512,128]{1,0:T(8,128)}, u32[]{:S(2)}) copy-start(s32[512,128]{1,0:T(8,128)} %kc_ref.1) | copy-start | bytes 786436
  2.9 0.9 %copy-start.1 = (s32[512,128]{1,0:T(8,128)S(1)}, s32[512,128]{1,0:T(8,128)}, u32[]{:S(2)}) copy-start(s32[512,128]{1,0:T(8,128)} %vc_ref.1) | copy-start | bytes 786436
  3.8 0.9 %copy-start.2 = (bf16[512,128]{1,0:T(8,128)(2,1)S(1)}, bf16[512,128]{1,0:T(8,128)(2,1)}, u32[]{:S(2)}) copy-start(bf16[512,128]{1,0:T(8,128)(2,1)} %q_ref.1) | copy-start | bytes 393220
  4.7 0.9 %copy-start.3 = (bf16[512,128]{1,0:T(8,128)(2,1)S(1)}, bf16[512,128]{1,0:T(8,128)(2,1)}, u32[]{:S(2)}) copy-start(bf16[512,128]{1,0:T(8,128)(2,1)} %g_ref.1) | copy-start | bytes 393220

commit v2 on v1

v2 whole, which is shorter than its diff:
```python
import functools
import math

import jax
import jax.numpy as jnp
from jax import lax
from jax.experimental import pallas as pl
from jax.experimental.pallas import tpu as pltpu
from jax.sharding import PartitionSpec as P

MESH = pl.DeviceIdType.MESH
LOW = jnp.bfloat16
WIDE = jnp.float32


def flipped(rank, step, count):
    total = 0
    bit = 1
    while bit < count:
        one = (rank // bit) % 2
        two = (step // bit) % 2
        total = total + bit * (one + two - 2 * one * two)
        bit *= 2
    return total


def contract(left, right, dims):
    return lax.dot_general(left, right, ((dims[:1], dims[1:]), ((), ())), preferred_element_type=WIDE)


def kernel(
    nq, nk, nka,
    key_scale, value_scale, q_ref, g_ref, kc_ref, vc_ref,
    dq_ref, dk_ref, dv_ref,
    qd, kv, codes, top, total, dot, stats, lse, delta, acc_q, acc_k, acc_v,
    gk_out, gk_in, gq_out, gq_in,
    load, q_send, q_recv, k_send, k_recv, s_send, s_recv, gk_send, gk_recv, gq_send, gq_recv,
):
    rows, width = q_ref.shape
    factor = 1.0 / math.sqrt(width)
    log2e = math.log2(math.e)
    pb, ka = lax.axis_index("pb"), lax.axis_index("ka")
    my_a, my_k = pb // nk, pb % nk
    my_q = my_a * nka + ka

    def q_rank(step):
        return flipped(my_q, step, nq)

    def k_rank(step):
        return flipped(my_k, step, nk)

    def q_peer(rank):
        return {"pb": (rank // nka) * nk + my_k, "ka": rank % nka}

    def k_peer(rank):
        return {"pb": my_a * nk + rank, "ka": ka}

    def q_copy(block, part, to, sem):
        b, t, s = q_rank(block), q_rank(to), q_rank(sem)
        return pltpu.make_async_remote_copy(
            qd.at[b, part], qd.at[b, part], q_send.at[s, part], q_recv.at[b, part],
            device_id=q_peer(t), device_id_type=MESH)

    def k_copy(block, part, to, sem):
        b, t, s = k_rank(block), k_rank(to), k_rank(sem)
        return pltpu.make_async_remote_copy(
            kv.at[b, part], kv.at[b, part], k_send.at[s, part], k_recv.at[b, part],
            device_id=k_peer(t), device_id_type=MESH)

    def s_copy(rank, slot):
        return pltpu.make_async_remote_copy(
            stats.at[slot], stats.at[slot], s_send.at[rank], s_recv.at[slot],
            device_id=q_peer(rank), device_id_type=MESH)

    def gk_copy(rank, slot):
        return pltpu.make_async_remote_copy(
            gk_out.at[rank], gk_in.at[slot], gk_send.at[rank], gk_recv.at[slot],
            device_id=k_peer(rank), device_id_type=MESH)

    def gq_copy(rank, slot):
        return pltpu.make_async_remote_copy(
            gq_out.at[rank], gq_in.at[slot], gq_send.at[rank], gq_recv.at[slot],
            device_id=q_peer(rank), device_id_type=MESH)

    loads = [
        pltpu.make_async_copy(q_ref, qd.at[my_q, 0], load.at[0]),
        pltpu.make_async_copy(g_ref, qd.at[my_q, 1], load.at[1]),
        pltpu.make_async_copy(kc_ref, codes.at[0], load.at[2]),
        pltpu.make_async_copy(vc_ref, codes.at[1], load.at[3]),
    ]
    for one in loads:
        one.start()
    barrier = pltpu.get_barrier_semaphore()
    for step in range(1, nq):
        pl.semaphore_signal(barrier, inc=1, device_id=q_peer(q_rank(step)), device_id_type=MESH)
    for step in range(1, nk):
        pl.semaphore_signal(barrier, inc=1, device_id=k_peer(k_rank(step)), device_id_type=MESH)
    for one in loads:
        one.wait()
    kv[my_k, 0] = (codes[0].astype(WIDE) * key_scale[0]).astype(LOW)
    kv[my_k, 1] = (codes[1].astype(WIDE) * value_scale[0]).astype(LOW)
    pl.semaphore_wait(barrier, nq + nk - 2)

    for part in range(2):
        q_copy(0, part, nka, nka).start()
        for step in range(2, nk, 2):
            k_copy(0, part, step, step).start()
        k_copy(0, part, 1, 1).start()
        for step in range(1, nka):
            q_copy(0, part, step, step).start()
    top[...] = jnp.full_like(top, -1e30)
    total[...] = jnp.zeros_like(total)
    dot[...] = jnp.zeros_like(dot)
    acc_q[...] = jnp.zeros_like(acc_q)
    acc_k[...] = jnp.zeros_like(acc_k)
    acc_v[...] = jnp.zeros_like(acc_v)

    def first(jj, ii):
        j, i = q_rank(jj), k_rank(ii)
        row = pl.ds(j, 1)
        scores = contract(kv[i, 0], qd[j, 0], (1, 1)) * (factor * log2e)
        d_probs = contract(kv[i, 1], qd[j, 1], (1, 1))
        old_top = top[row, :]
        new_top = jnp.maximum(old_top, jnp.max(scores, axis=0, keepdims=True))
        shifted = jnp.exp2(scores - new_top)
        old = jnp.exp2(old_top - new_top)
        total[row, :] = total[row, :] * old + jnp.sum(shifted, axis=0, keepdims=True)
        dot[row, :] = dot[row, :] * old + jnp.sum(shifted * d_probs, axis=0, keepdims=True)
        top[row, :] = new_top

    def first_over(j_range, i_range):
        if len(j_range) * len(i_range) == 0:
            return

        @pl.loop(0, len(j_range) * len(i_range))
        def _(n):
            first(
                j_range.start + n // len(i_range) * j_range.step,
                i_range.start + n % len(i_range) * i_range.step,
            )

    first_over(range(0, 1), range(0, 1))
    for part in range(2):
        k_copy(1, part, 1, 1).wait_recv()
    first_over(range(0, 1), range(1, 2))
    for step in range(1, nka):
        for part in range(2):
            q_copy(step, part, step, step).wait_recv()
    first_over(range(1, nka), range(0, 2))
    for part in range(2):
        q_copy(nka, part, nka, nka).wait_recv()
        for step in range(1, nka):
            q_copy(nka, part, step, nka + step).start()
        for step in range(2, nk, 2):
            k_copy(step, part, step, step).wait_recv()
            k_copy(step, part, 1, step + 1).start()
    first_over(range(0, nka + 1), range(2, nk, 2))
    first_over(range(nka, nka + 1), range(0, 2))
    for step in range(3, nk, 2):
        for part in range(2):
            k_copy(step, part, step, step).wait_recv()
    first_over(range(0, nka + 1), range(3, nk, 2))
    for step in range(nka + 1, nq):
        for part in range(2):
            q_copy(step, part, step, step).wait_recv()
    first_over(range(nka + 1, nq), range(0, nk))

    stats[my_q, 0:nq, :] = top[...] + jnp.log2(total[...])
    stats[my_q, nq : 2 * nq, :] = dot[...] / total[...]
    for step in range(1, nq):
        s_copy(q_rank(nq - step), my_q).start()
    for step in range(1, nq):
        other = q_rank(step)
        s_copy(other, other).wait_recv()
    parts = [stats[r, 0:nq, :] for r in range(nq)]
    best = functools.reduce(jnp.maximum, parts)
    weights = [jnp.exp2(part - best) for part in parts]
    whole = sum(weights)
    lse[...] = best + jnp.log2(whole)
    delta[...] = sum(w * stats[r, nq : 2 * nq, :] for r, w in enumerate(weights)) / whole

    def second(jj, ii):
        j, i = q_rank(jj), k_rank(ii)
        keys, queries, grads = kv[i, 0], qd[j, 0], qd[j, 1]
        scores = contract(keys, queries, (1, 1)) * (factor * log2e)
        d_probs = contract(kv[i, 1], grads, (1, 1))
        probs = jnp.exp2(scores - lse[pl.ds(j, 1), :])
        d_scores = (probs * (d_probs - delta[pl.ds(j, 1), :])).astype(LOW)
        acc_v[i] += contract(probs.astype(LOW), grads, (1, 0))
        acc_k[i] += contract(d_scores, queries, (1, 0))
        acc_q[j] += contract(d_scores, keys, (0, 0))

    def send_keys(ii):
        i = k_rank(ii)
        gk_out[i, 0] = (acc_k[i] * factor).astype(LOW)
        gk_out[i, 1] = acc_v[i].astype(LOW)
        gk_copy(i, my_k).start()

    def send_queries(jj):
        j = q_rank(jj)
        gq_out[j] = (acc_q[j] * factor).astype(LOW)
        gq_copy(j, my_q).start()

    @pl.loop(0, nk - 2)
    def _(n):
        ii = nk - 1 - n

        @pl.loop(0, nq)
        def _(jj):
            second(jj, ii)

        send_keys(ii)

    @pl.loop(0, nq - nka)
    def _(n):
        jj = nq - 1 - n

        @pl.loop(0, 2)
        def _(m):
            second(jj, 1 - m)

        send_queries(jj)

    @pl.loop(0, 2 * nka)
    def _(n):
        jj = nka - 1 - n % nka
        second(jj, 1 - n // nka)

        @pl.when(n == nka - 1)
        def _():
            send_keys(1)

        @pl.when((n >= nka) & (jj > 0))
        def _():
            send_queries(jj)

    key_sum, value_sum = acc_k[my_k] * factor, acc_v[my_k]
    for step in range(nk - 1, 0, -1):
        other = k_rank(step)
        gk_copy(other, other).wait_recv()
        key_sum = key_sum + gk_in[other, 0].astype(WIDE)
        value_sum = value_sum + gk_in[other, 1].astype(WIDE)
    dk_ref[...] = key_sum
    dv_ref[...] = value_sum
    query_sum = acc_q[my_q] * factor
    for step in range(nq - 1, 0, -1):
        other = q_rank(step)
        gq_copy(other, other).wait_recv()
        query_sum = query_sum + gq_in[other].astype(WIDE)
    dq_ref[...] = query_sum
    for step in range(1, nq):
        other = q_rank(step)
        for part in range(2):
            q_copy(0, part, step, step).wait_send()
        s_copy(other, my_q).wait_send()
        gq_copy(other, my_q).wait_send()
    for step in range(1, nk):
        other = k_rank(step)
        for part in range(2):
            k_copy(0, part, step, step).wait_send()
        gk_copy(other, my_k).wait_send()


def shards(queries, key_codes, value_codes, key_scale, value_scale, out_grad):
    rows, width = queries.shape
    npb, nka = lax.axis_size("pb"), lax.axis_size("ka")
    nq, nk = 2 * nka, npb // 2
    vmem = pl.BlockSpec(memory_space=pltpu.VMEM)
    hbm = pl.BlockSpec(memory_space=pltpu.HBM)
    smem = pl.BlockSpec(memory_space=pltpu.SMEM)
    out = jax.ShapeDtypeStruct((rows, width), WIDE)
    counts = ((4,), (nq, 2), (nq, 2), (nk, 2), (nk, 2), (nq,), (nq,), (nk,), (nk,), (nq,), (nq,))
    sems = [pltpu.SemaphoreType.DMA(count) for count in counts]
    return tuple(
        pl.pallas_call(
            functools.partial(kernel, nq, nk, nka),
            out_shape=(out, out, out),
            in_specs=[smem, smem, hbm, hbm, hbm, hbm],
            out_specs=(vmem, vmem, vmem),
            scratch_shapes=[
                pltpu.VMEM((nq, 2, rows, width), LOW),
                pltpu.VMEM((nk, 2, rows, width), LOW),
                pltpu.VMEM((2, rows, width), jnp.int32),
                pltpu.VMEM((nq, rows), WIDE),
                pltpu.VMEM((nq, rows), WIDE),
                pltpu.VMEM((nq, rows), WIDE),
                pltpu.VMEM((nq, 2 * nq, rows), WIDE),
                pltpu.VMEM((nq, rows), WIDE),
                pltpu.VMEM((nq, rows), WIDE),
                pltpu.VMEM((nq, rows, width), WIDE),
                pltpu.VMEM((nk, rows, width), WIDE),
                pltpu.VMEM((nk, rows, width), WIDE),
                pltpu.VMEM((nk, 2, rows, width), LOW),
                pltpu.VMEM((nk, 2, rows, width), LOW),
                pltpu.VMEM((nq, rows, width), LOW),
                pltpu.VMEM((nq, rows, width), LOW),
                *sems,
            ],
            compiler_params=pltpu.CompilerParams(
                collective_id=0, has_side_effects=True, vmem_limit_bytes=60 << 20
            ),
        )(key_scale.reshape(1), value_scale.reshape(1), queries, out_grad, key_codes, value_codes)
    )


def solution(mesh):
    in_specs = (
        P(("pb", "ka"), "ha"),
        P(("ka", "pb"), "ha"),
        P(("ka", "pb"), "ha"),
        P(),
        P(),
        P(("pb", "ka"), "ha"),
    )
    out_specs = (P(("pb", "ka"), "ha"), P(("ka", "pb"), "ha"), P(("ka", "pb"), "ha"))
    return jax.shard_map(shards, mesh=mesh, in_specs=in_specs, out_specs=out_specs, check_vma=False)
```

time: 65.4 us -> 59.2 us (0.905)
  Pallas kernels: 57.4 us -> 53.6 us
  local copies, waits for them, and re-layouts: 5.81 us -> 3.46 us
    pallas_call x1, Pallas kernels: 57.4 us -> 53.6 us  [shards(): pl.pallas_call(functools.partial(kernel, nq, nk, nka), out_shape=(out, ou...]
    unnamed x11 -> x7, local copies, waits for them, and re-layouts: 5.81 us -> 3.46 us
where the time goes in v2:
time: 59.2 us; the launch traced here: 59 us
  Pallas kernels  53.6 us (91%)
  local copies, waits for them, and re-layouts  3.46 us (6%)
  between operations  1.94 us (3%)
    pallas_call x1, Pallas kernels, shards(): pl.pallas_call(functools.partial(kernel, nq, nk, nka), out_shape=(out, ou...  53.6 us
    unnamed x7, local copies, waits for them, and re-layouts  3.46 us

profile of v2, /device:TPU:0, one launch (start us, length us, event | category | flops | bytes accessed | tf_op | source)
XLA Modules:
  0.0 59.0 jit_solution(4101127469190564427)
XLA Ops:
  1.9 53.6 %shard_map.85 = (f32[512,128]{1,0:T(8,128)}, f32[512,128]{1,0:T(8,128)}, f32[512,128]{1,0:T(8,128)}) custom-call(f32[1]{0:T(128)} %bitcast.2.key_scale, f32[1]{0:T(128)} %bitcast.3.value_scale, bf16[512,128]{1,0:T(8,128)(2,1)} %q_ref.1, bf16[512,128]{1,0:T(8,128)(2,1)} %g_ref.1, s32[512,128]{1,0:T(8,128)} %kc_ref.1, s32[512,128]{1,0:T(8,128)} %vc_ref.1), custom_call_target="tpu_custom_call" | custom-call | tf_op jit(solution)/shard_map/pallas_call | solution.py:275
  55.6 0.0 copy-start.1
  55.6 1.7 %copy.14 = f32[512,128]{1,0:T(8,128)} copy(f32[512,128]{1,0:T(8,128)} %get-tuple-element.6) | data formatting | bytes 524288
  57.3 0.0 copy-done.1
  57.3 0.0 copy-start
  57.3 0.7 %copy.15 = f32[512,128]{1,0:T(8,128)} copy(f32[512,128]{1,0:T(8,128)S(1)} %copy-done.1) | data formatting | bytes 524288
  58.0 0.3 copy-done
  58.3 0.7 %copy.16 = f32[512,128]{1,0:T(8,128)} copy(f32[512,128]{1,0:T(8,128)S(1)} %copy-done) | data formatting | bytes 524288
Async XLA Ops:
  55.6 1.7 %copy-start.1 = (f32[512,128]{1,0:T(8,128)S(1)}, f32[512,128]{1,0:T(8,128)}, u32[]{:S(2)}) copy-start(f32[512,128]{1,0:T(8,128)} %get-tuple-element.7) | copy-start | bytes 786436
  57.3 1.0 %copy-start = (f32[512,128]{1,0:T(8,128)S(1)}, f32[512,128]{1,0:T(8,128)}, u32[]{:S(2)}) copy-start(f32[512,128]{1,0:T(8,128)} %get-tuple-element.8) | copy-start | bytes 786436

commit v3 on v2

--- a/solution.py
+++ b/solution.py
@@ -10,6 +10,7 @@
 
 MESH = pl.DeviceIdType.MESH
 LOW = jnp.bfloat16
+PARTS = 4
 WIDE = jnp.float32
 
 
@@ -33,8 +34,9 @@
     key_scale, value_scale, q_ref, g_ref, kc_ref, vc_ref,
     dq_ref, dk_ref, dv_ref,
     qd, kv, codes, top, total, dot, stats, lse, delta, acc_q, acc_k, acc_v,
-    gk_out, gk_in, gq_out, gq_in,
-    load, q_send, q_recv, k_send, k_recv, s_send, s_recv, gk_send, gk_recv, gq_send, gq_recv,
+    gk_out, gk_mid, gk_in, gq_out, gq_mid, gq_in,
+    load, q_send, q_recv, k_send, k_recv, s_send, s_recv,
+    gk_send, gk_mid_recv, gk_recv, gq_send, gq_mid_recv, gq_recv,
 ):
     rows, width = q_ref.shape
     factor = 1.0 / math.sqrt(width)
@@ -55,16 +57,21 @@
     def k_peer(rank):
         return {"pb": my_a * nk + rank, "ka": ka}
 
+    def span(part):
+        return pl.ds(part % 2 * (rows // 2), rows // 2)
+
     def q_copy(block, part, to, sem):
         b, t, s = q_rank(block), q_rank(to), q_rank(sem)
         return pltpu.make_async_remote_copy(
-            qd.at[b, part], qd.at[b, part], q_send.at[s, part], q_recv.at[b, part],
+            qd.at[b, part // 2, span(part)], qd.at[b, part // 2, span(part)],
+            q_send.at[s, part], q_recv.at[b, part],
             device_id=q_peer(t), device_id_type=MESH)
 
     def k_copy(block, part, to, sem):
         b, t, s = k_rank(block), k_rank(to), k_rank(sem)
         return pltpu.make_async_remote_copy(
-            kv.at[b, part], kv.at[b, part], k_send.at[s, part], k_recv.at[b, part],
+            kv.at[b, part // 2, span(part)], kv.at[b, part // 2, span(part)],
+            k_send.at[s, part], k_recv.at[b, part],
             device_id=k_peer(t), device_id_type=MESH)
 
     def s_copy(rank, slot):
@@ -77,10 +84,20 @@
             gk_out.at[rank], gk_in.at[slot], gk_send.at[rank], gk_recv.at[slot],
             device_id=k_peer(rank), device_id_type=MESH)
 
+    def gk_mid_copy(rank):
+        return pltpu.make_async_remote_copy(
+            gk_out.at[rank], gk_mid.at[rank], gk_send.at[rank], gk_mid_recv.at[rank],
+            device_id=k_peer(k_rank(1)), device_id_type=MESH)
+
     def gq_copy(rank, slot):
         return pltpu.make_async_remote_copy(
             gq_out.at[rank], gq_in.at[slot], gq_send.at[rank], gq_recv.at[slot],
             device_id=q_peer(rank), device_id_type=MESH)
+
+    def gq_mid_copy(step, slot):
+        return pltpu.make_async_remote_copy(
+            gq_out.at[q_rank(step)], gq_mid.at[slot], gq_send.at[q_rank(step)], gq_mid_recv.at[slot],
+            device_id=q_peer(q_rank(step - nka)), device_id_type=MESH)
 
     loads = [
         pltpu.make_async_copy(q_ref, qd.at[my_q, 0], load.at[0]),
@@ -101,7 +118,7 @@
     kv[my_k, 1] = (codes[1].astype(WIDE) * value_scale[0]).astype(LOW)
     pl.semaphore_wait(barrier, nq + nk - 2)
 
-    for part in range(2):
+    for part in range(PARTS):
         q_copy(0, part, nka, nka).start()
         for step in range(2, nk, 2):
             k_copy(0, part, step, step).start()
@@ -139,29 +156,34 @@
                 i_range.start + n % len(i_range) * i_range.step,
             )
 
-    first_over(range(0, 1), range(0, 1))
-    for part in range(2):
-        k_copy(1, part, 1, 1).wait_recv()
-    first_over(range(0, 1), range(1, 2))
-    for step in range(1, nka):
-        for part in range(2):
-            q_copy(step, part, step, step).wait_recv()
-    first_over(range(1, nka), range(0, 2))
-    for part in range(2):
+    def forward(part):
         q_copy(nka, part, nka, nka).wait_recv()
         for step in range(1, nka):
             q_copy(nka, part, step, nka + step).start()
         for step in range(2, nk, 2):
             k_copy(step, part, step, step).wait_recv()
             k_copy(step, part, 1, step + 1).start()
+
+    first_over(range(0, 1), range(0, 1))
+    forward(0)
+    for part in range(PARTS):
+        k_copy(1, part, 1, 1).wait_recv()
+    first_over(range(0, 1), range(1, 2))
+    forward(1)
+    for step in range(1, nka):
+        for part in range(PARTS):
+            q_copy(step, part, step, step).wait_recv()
+    first_over(range(1, nka), range(0, 2))
+    for part in range(2, PARTS):
+        forward(part)
     first_over(range(0, nka + 1), range(2, nk, 2))
     first_over(range(nka, nka + 1), range(0, 2))
     for step in range(3, nk, 2):
-        for part in range(2):
+        for part in range(PARTS):
             k_copy(step, part, step, step).wait_recv()
     first_over(range(0, nka + 1), range(3, nk, 2))
     for step in range(nka + 1, nq):
-        for part in range(2):
+        for part in range(PARTS):
             q_copy(step, part, step, step).wait_recv()
     first_over(range(nka + 1, nq), range(0, nk))
 
@@ -190,36 +212,57 @@
         acc_k[i] += contract(d_scores, queries, (1, 0))
         acc_q[j] += contract(d_scores, keys, (0, 0))
 
-    def send_keys(ii):
-        i = k_rank(ii)
+    def pack_keys(i):
         gk_out[i, 0] = (acc_k[i] * factor).astype(LOW)
         gk_out[i, 1] = acc_v[i].astype(LOW)
-        gk_copy(i, my_k).start()
-
-    def send_queries(jj):
-        j = q_rank(jj)
+
+    def pack_queries(j):
         gq_out[j] = (acc_q[j] * factor).astype(LOW)
-        gq_copy(j, my_q).start()
-
-    @pl.loop(0, nk - 2)
+
+    @pl.loop(0, nk // 2 - 1)
     def _(n):
-        ii = nk - 1 - n
+        ii = nk - 1 - 2 * n
 
         @pl.loop(0, nq)
         def _(jj):
             second(jj, ii)
 
-        send_keys(ii)
+        pack_keys(k_rank(ii))
+        gk_mid_copy(k_rank(ii)).start()
 
     @pl.loop(0, nq - nka)
     def _(n):
         jj = nq - 1 - n
 
-        @pl.loop(0, 2)
+        @pl.loop(0, nk // 2 + 1)
         def _(m):
-            second(jj, 1 - m)
-
-        send_queries(jj)
+            second(jj, 2 * (m - 1) + 3 * ((nk // 2 + 1 - m) // (nk // 2 + 1)))
+
+        @pl.when(jj > nka)
+        def _():
+            pack_queries(q_rank(jj))
+            gq_mid_copy(jj, my_q).start()
+
+    far = q_rank(nka)
+    query_sum = acc_q[far] * factor
+    for step in range(1, nka):
+        gq_mid_copy(nka + step, q_rank(step)).wait_recv()
+        query_sum = query_sum + gq_mid[q_rank(step)].astype(WIDE)
+    gq_out[far] = query_sum.astype(LOW)
+    gq_copy(far, my_q).start()
+
+    @pl.loop(0, nk // 2 - 1)
+    def _(n):
+        i = k_rank(2 + 2 * n)
+
+        @pl.loop(0, nka)
+        def _(jj):
+            second(jj, 2 + 2 * n)
+
+        gk_mid_copy(i).wait_recv()
+        gk_out[i, 0] = (acc_k[i] * factor + gk_mid[i, 0].astype(WIDE)).astype(LOW)
+        gk_out[i, 1] = (acc_v[i] + gk_mid[i, 1].astype(WIDE)).astype(LOW)
+        gk_copy(i, my_k).start()
 
     @pl.loop(0, 2 * nka)
     def _(n):
@@ -228,35 +271,37 @@
 
         @pl.when(n == nka - 1)
         def _():
-            send_keys(1)
+            pack_keys(k_rank(1))
+            gk_copy(k_rank(1), my_k).start()
 
         @pl.when((n >= nka) & (jj > 0))
         def _():
-            send_queries(jj)
-
+            pack_queries(q_rank(jj))
+            gq_copy(q_rank(jj), my_q).start()
+
+    query_sum = acc_q[my_q] * factor
+    for step in range(nka, 0, -1):
+        other = q_rank(step)
+        gq_copy(other, other).wait_recv()
+        query_sum = query_sum + gq_in[other].astype(WIDE)
+    dq_ref[...] = query_sum
     key_sum, value_sum = acc_k[my_k] * factor, acc_v[my_k]
-    for step in range(nk - 1, 0, -1):
+    for step in (*range(2, nk, 2), 1):
         other = k_rank(step)
         gk_copy(other, other).wait_recv()
         key_sum = key_sum + gk_in[other, 0].astype(WIDE)
         value_sum = value_sum + gk_in[other, 1].astype(WIDE)
     dk_ref[...] = key_sum
     dv_ref[...] = value_sum
-    query_sum = acc_q[my_q] * factor
-    for step in range(nq - 1, 0, -1):
-        other = q_rank(step)
-        gq_copy(other, other).wait_recv()
-        query_sum = query_sum + gq_in[other].astype(WIDE)
-    dq_ref[...] = query_sum
     for step in range(1, nq):
         other = q_rank(step)
-        for part in range(2):
+        for part in range(PARTS):
             q_copy(0, part, step, step).wait_send()
         s_copy(other, my_q).wait_send()
         gq_copy(other, my_q).wait_send()
     for step in range(1, nk):
         other = k_rank(step)
-        for part in range(2):
+        for part in range(PARTS):
             k_copy(0, part, step, step).wait_send()
         gk_copy(other, my_k).wait_send()
 
@@ -269,7 +314,7 @@
     hbm = pl.BlockSpec(memory_space=pltpu.HBM)
     smem = pl.BlockSpec(memory_space=pltpu.SMEM)
     out = jax.ShapeDtypeStruct((rows, width), WIDE)
-    counts = ((4,), (nq, 2), (nq, 2), (nk, 2), (nk, 2), (nq,), (nq,), (nk,), (nk,), (nq,), (nq,))
+    counts = ((4,), *[(n, PARTS) for n in (nq, nq, nk, nk)], *[(n,) for n in (nq, nq, nk, nk, nk, nq, nq, nq)])
     sems = [pltpu.SemaphoreType.DMA(count) for count in counts]
     return tuple(
         pl.pallas_call(
@@ -290,10 +335,8 @@
                 pltpu.VMEM((nq, rows, width), WIDE),
                 pltpu.VMEM((nk, rows, width), WIDE),
                 pltpu.VMEM((nk, rows, width), WIDE),
-                pltpu.VMEM((nk, 2, rows, width), LOW),
-                pltpu.VMEM((nk, 2, rows, width), LOW),
-                pltpu.VMEM((nq, rows, width), LOW),
-                pltpu.VMEM((nq, rows, width), LOW),
+                *[pltpu.VMEM((nk, 2, rows, width), LOW)] * 3,
+                *[pltpu.VMEM((nq, rows, width), LOW)] * 3,
                 *sems,
             ],
             compiler_params=pltpu.CompilerParams(

time: 59.2 us -> 57 us (0.963)
  Pallas kernels: 53.6 us -> 51.4 us
    pallas_call x1, Pallas kernels: 53.6 us -> 51.4 us  [shards(): pl.pallas_call(functools.partial(kernel, nq, nk, nka), out_shape=(out, ou...]
where the time goes in v3:
time: 57 us; the launch traced here: 56.8 us
  Pallas kernels  51.4 us (90%)
  local copies, waits for them, and re-layouts  3.46 us (6%)
  between operations  1.94 us (3%)
    pallas_call x1, Pallas kernels, shards(): pl.pallas_call(functools.partial(kernel, nq, nk, nka), out_shape=(out, ou...  51.4 us
    unnamed x7, local copies, waits for them, and re-layouts  3.46 us

profile of v3, /device:TPU:0, one launch (start us, length us, event | category | flops | bytes accessed | tf_op | source)
XLA Modules:
  0.0 56.8 jit_solution(14396300486079130895)
XLA Ops:
  1.9 51.4 %shard_map.85 = (f32[512,128]{1,0:T(8,128)}, f32[512,128]{1,0:T(8,128)}, f32[512,128]{1,0:T(8,128)}) custom-call(f32[1]{0:T(128)} %bitcast.2.key_scale, f32[1]{0:T(128)} %bitcast.3.value_scale, bf16[512,128]{1,0:T(8,128)(2,1)} %q_ref.1, bf16[512,128]{1,0:T(8,128)(2,1)} %g_ref.1, s32[512,128]{1,0:T(8,128)} %kc_ref.1, s32[512,128]{1,0:T(8,128)} %vc_ref.1), custom_call_target="tpu_custom_call" | custom-call | tf_op jit(solution)/shard_map/pallas_call | solution.py:320
  53.3 0.0 copy-start.1
  53.3 1.7 %copy.14 = f32[512,128]{1,0:T(8,128)} copy(f32[512,128]{1,0:T(8,128)} %get-tuple-element.6) | data formatting | bytes 524288
  55.0 0.0 copy-done.1
  55.0 0.0 copy-start
  55.0 0.7 %copy.15 = f32[512,128]{1,0:T(8,128)} copy(f32[512,128]{1,0:T(8,128)S(1)} %copy-done.1) | data formatting | bytes 524288
  55.7 0.3 copy-done
  56.1 0.7 %copy.16 = f32[512,128]{1,0:T(8,128)} copy(f32[512,128]{1,0:T(8,128)S(1)} %copy-done) | data formatting | bytes 524288
Async XLA Ops:
  53.3 1.7 %copy-start.1 = (f32[512,128]{1,0:T(8,128)S(1)}, f32[512,128]{1,0:T(8,128)}, u32[]{:S(2)}) copy-start(f32[512,128]{1,0:T(8,128)} %get-tuple-element.7) | copy-start | bytes 786436
  55.0 1.0 %copy-start = (f32[512,128]{1,0:T(8,128)S(1)}, f32[512,128]{1,0:T(8,128)}, u32[]{:S(2)}) copy-start(f32[512,128]{1,0:T(8,128)} %get-tuple-element.8) | copy-start | bytes 786436

commit v4 on v3

--- a/solution.py
+++ b/solution.py
@@ -210,20 +210,20 @@
         d_scores = (probs * (d_probs - delta[pl.ds(j, 1), :])).astype(LOW)
         acc_v[i] += contract(probs.astype(LOW), grads, (1, 0))
         acc_k[i] += contract(d_scores, queries, (1, 0))
-        acc_q[j] += contract(d_scores, keys, (0, 0))
+        acc_q[j] += contract(keys, d_scores, (0, 0))
 
     def pack_keys(i):
         gk_out[i, 0] = (acc_k[i] * factor).astype(LOW)
         gk_out[i, 1] = acc_v[i].astype(LOW)
 
     def pack_queries(j):
-        gq_out[j] = (acc_q[j] * factor).astype(LOW)
+        gq_out[j] = (acc_q[j].T * factor).astype(LOW)
 
     @pl.loop(0, nk // 2 - 1)
     def _(n):
         ii = nk - 1 - 2 * n
 
-        @pl.loop(0, nq)
+        @pl.loop(0, nq, unroll=2)
         def _(jj):
             second(jj, ii)
 
@@ -244,7 +244,7 @@
             gq_mid_copy(jj, my_q).start()
 
     far = q_rank(nka)
-    query_sum = acc_q[far] * factor
+    query_sum = acc_q[far].T * factor
     for step in range(1, nka):
         gq_mid_copy(nka + step, q_rank(step)).wait_recv()
         query_sum = query_sum + gq_mid[q_rank(step)].astype(WIDE)
@@ -255,7 +255,7 @@
     def _(n):
         i = k_rank(2 + 2 * n)
 
-        @pl.loop(0, nka)
+        @pl.loop(0, nka, unroll=2)
         def _(jj):
             second(jj, 2 + 2 * n)
 
@@ -279,7 +279,7 @@
             pack_queries(q_rank(jj))
             gq_copy(q_rank(jj), my_q).start()
 
-    query_sum = acc_q[my_q] * factor
+    query_sum = acc_q[my_q].T * factor
     for step in range(nka, 0, -1):
         other = q_rank(step)
         gq_copy(other, other).wait_recv()
@@ -332,7 +332,7 @@
                 pltpu.VMEM((nq, 2 * nq, rows), WIDE),
                 pltpu.VMEM((nq, rows), WIDE),
                 pltpu.VMEM((nq, rows), WIDE),
-                pltpu.VMEM((nq, rows, width), WIDE),
+                pltpu.VMEM((nq, width, rows), WIDE),
                 pltpu.VMEM((nk, rows, width), WIDE),
                 pltpu.VMEM((nk, rows, width), WIDE),
                 *[pltpu.VMEM((nk, 2, rows, width), LOW)] * 3,

time: 57 us -> 56.3 us (0.988)
  Pallas kernels: 51.4 us -> 50.7 us
    pallas_call x1, Pallas kernels: 51.4 us -> 50.7 us  [shards(): pl.pallas_call(functools.partial(kernel, nq, nk, nka), out_shape=(out, ou...]
where the time goes in v4:
time: 56.3 us; the launch traced here: 56.1 us
  Pallas kernels  50.7 us (90%)
  local copies, waits for them, and re-layouts  3.46 us (6%)
  between operations  1.94 us (3%)
    pallas_call x1, Pallas kernels, shards(): pl.pallas_call(functools.partial(kernel, nq, nk, nka), out_shape=(out, ou...  50.7 us
    unnamed x7, local copies, waits for them, and re-layouts  3.46 us

profile of v4, /device:TPU:0, one launch (start us, length us, event | category | flops | bytes accessed | tf_op | source)
XLA Modules:
  0.0 56.1 jit_solution(7028879775405989600)
XLA Ops:
  1.9 50.7 %shard_map.85 = (f32[512,128]{1,0:T(8,128)}, f32[512,128]{1,0:T(8,128)}, f32[512,128]{1,0:T(8,128)}) custom-call(f32[1]{0:T(128)} %bitcast.2.key_scale, f32[1]{0:T(128)} %bitcast.3.value_scale, bf16[512,128]{1,0:T(8,128)(2,1)} %q_ref.1, bf16[512,128]{1,0:T(8,128)(2,1)} %g_ref.1, s32[512,128]{1,0:T(8,128)} %kc_ref.1, s32[512,128]{1,0:T(8,128)} %vc_ref.1), custom_call_target="tpu_custom_call" | custom-call | tf_op jit(solution)/shard_map/pallas_call | solution.py:320
  52.6 0.0 copy-start.1
  52.6 1.7 %copy.14 = f32[512,128]{1,0:T(8,128)} copy(f32[512,128]{1,0:T(8,128)} %get-tuple-element.6) | data formatting | bytes 524288
  54.3 0.0 copy-done.1
  54.3 0.0 copy-start
  54.3 0.7 %copy.15 = f32[512,128]{1,0:T(8,128)} copy(f32[512,128]{1,0:T(8,128)S(1)} %copy-done.1) | data formatting | bytes 524288
  55.0 0.3 copy-done
  55.4 0.7 %copy.16 = f32[512,128]{1,0:T(8,128)} copy(f32[512,128]{1,0:T(8,128)S(1)} %copy-done) | data formatting | bytes 524288
Async XLA Ops:
  52.6 1.7 %copy-start.1 = (f32[512,128]{1,0:T(8,128)S(1)}, f32[512,128]{1,0:T(8,128)}, u32[]{:S(2)}) copy-start(f32[512,128]{1,0:T(8,128)} %get-tuple-element.7) | copy-start | bytes 786436
  54.3 1.0 %copy-start = (f32[512,128]{1,0:T(8,128)S(1)}, f32[512,128]{1,0:T(8,128)}, u32[]{:S(2)}) copy-start(f32[512,128]{1,0:T(8,128)} %get-tuple-element.8) | copy-start | bytes 786436
